TPU v7x, 256 devices: a whole 4x4x8 slice. The times are simulated.
256 devices in a mesh: req: 32 (over x, y, core), tp: 8 (over z).
Axes of the slice: x: 4, y: 4, z: 8, core: 2. Of those that a mesh axis runs over, the one named last changes fastest.
Arguments:
- queries: bfloat16 [4096, 8192], P('req', 'tp'), may hold values from -80 to 80
- incoming_key_value: bfloat16 [2, 4096, 1024], P(None, 'req', 'tp'), may hold values from -4 to 4
- key_value_pages: bfloat16 [16384, 32, 2, 1024], P('req', None, None, 'tp'), may hold values from -4 to 4
- page_request_home: int32 [16384], P('req'), may hold values from 0 to 16383, as said below
- lengths: int32 [1024], P('req'), may hold values from 1 to 512, 262144 in all
- request_adapter_index: int32 [1024], P('req'), may hold values from 0 to 63
- adapter_storage_slot: int32 [64], replicated, may hold values from 0 to 63, each once
- adapter_down_factor: bfloat16 [64, 8192, 64], P('req', 'tp'), may hold values from -0.25 to 0.25
- adapter_up_factor: bfloat16 [64, 64, 8192], P('req'), may hold values from -0.75 to 0.75
- output_projection_weight: bfloat16 [8192, 8192], P('tp', 'req'), may hold values from -0.75 to 0.75
Outputs:
- attn_out: bfloat16 [4096, 8192], P('tp', 'req')
Inputs may be any that keep to these rules, and one draw needn't show every extreme that they name: `page_request_home`: each value once. Pages p with p // 512 = a hold pages of requests i with i // 32 = b, b != a, for at most 2 pages p for every pair a, b; in every draw some a holds exactly 2 pages of every b != a.
All inputs are finite; a program needn't handle non-finite values. No bound on the sum of `lengths` on one device may be relied on, other than what follows from the above.
Results may differ from a plain program's by a relative error of at most 0.0058.
Values may be sent and summed in bfloat16 or wider, within the bound.
A program may use at most 128 MiB of HBM per device.

v0:
```python
import math
import jax
import jax.numpy as jnp
from jax import lax
from jax.sharding import PartitionSpec as P

QUERY_HEADS = 64
KEY_VALUE_HEADS = 8
HEAD_WIDTH = 128
STEP_COUNT = 4
PAGE_LENGTH = 32
MAXP = 16
CAP = 2


def relocate(key_value_pages, page_request_home, my_req, req_count):
    per_dev = key_value_pages.shape[0]
    destination = page_request_home // per_dev
    remote = destination != my_req
    matches = (destination[:, None] == jnp.arange(req_count, dtype=jnp.int32)[None, :]) & remote[
        :, None
    ]
    before = jnp.cumsum(matches.astype(jnp.int32), axis=0) - 1
    placing = jnp.sum(jnp.where(matches, before, 0), axis=1)
    target = jnp.where(remote, destination * CAP + placing, req_count * CAP)
    page_numbers = jnp.arange(per_dev, dtype=jnp.int32)
    out_match = target[:, None] == jnp.arange(req_count * CAP, dtype=jnp.int32)[None, :]
    filled = jnp.any(out_match, axis=0)
    out_source = jnp.sum(jnp.where(out_match, page_numbers[:, None], 0), axis=0)
    out_label = jnp.sum(jnp.where(out_match, page_request_home[:, None], 0), axis=0)
    picked = jnp.take(key_value_pages, out_source, axis=0)
    outbox = jnp.where(filled[:, None, None, None], picked, jnp.zeros((), key_value_pages.dtype))
    labels = jnp.where(filled, out_label, -1)
    inbox_pages, arrived = (
        lax.all_to_all(outbox, "req", split_axis=0, concat_axis=0, tiled=True),
        lax.all_to_all(labels, "req", split_axis=0, concat_axis=0, tiled=True),
    )
    own_label = jnp.where(remote, -1, page_request_home - my_req * per_dev)
    in_label = jnp.where(arrived >= 0, arrived - my_req * per_dev, -1)
    candidate_label = jnp.concatenate([own_label, in_label], axis=0)
    candidates = jnp.concatenate([key_value_pages, inbox_pages], axis=0)
    candidate_numbers = jnp.arange(candidate_label.shape[0], dtype=jnp.int32)
    slot_match = candidate_label[:, None] == page_numbers[None, :]
    slot_source = jnp.sum(jnp.where(slot_match, candidate_numbers[:, None], 0), axis=0)
    return jnp.take(candidates, slot_source, axis=0)


def attend(queries, incoming_key_value, cache_pages, lengths):
    heads_kv = cache_pages.shape[-1] // HEAD_WIDTH
    query_group_count = QUERY_HEADS // KEY_VALUE_HEADS
    requests = lengths.shape[0]
    cache_extent = MAXP * PAGE_LENGTH
    score_scale = 1.0 / math.sqrt(HEAD_WIDTH)
    stored_entries = cache_pages.reshape(requests, cache_extent, 2, heads_kv, HEAD_WIDTH)
    fresh_key_value = incoming_key_value.reshape(2, requests, STEP_COUNT, heads_kv, HEAD_WIDTH)
    query_vectors = queries.reshape(requests, STEP_COUNT, heads_kv, query_group_count, HEAD_WIDTH)
    old_scores = (
        jnp.einsum(
            "rsgqd,rlgd->rgqsl",
            query_vectors,
            stored_entries[:, :, 0],
            preferred_element_type=jnp.float32,
        )
        * score_scale
    )
    new_scores = (
        jnp.einsum(
            "rsgqd,rtgd->rgqst",
            query_vectors,
            fresh_key_value[0],
            preferred_element_type=jnp.float32,
        )
        * score_scale
    )
    keep_old = jnp.arange(cache_extent, dtype=jnp.int32)[None, :] < lengths[:, None]
    keep_new = jnp.arange(STEP_COUNT)[None, :] <= jnp.arange(STEP_COUNT)[:, None]
    old_scores = jnp.where(keep_old[:, None, None, None, :], old_scores, -jnp.inf)
    new_scores = jnp.where(keep_new[None, None, None], new_scores, -jnp.inf)
    row_top = jnp.maximum(jnp.max(old_scores, axis=-1), jnp.max(new_scores, axis=-1))
    old_weights = jnp.exp(old_scores - row_top[..., None])
    new_weights = jnp.exp(new_scores - row_top[..., None])
    totals = jnp.sum(old_weights, axis=-1) + jnp.sum(new_weights, axis=-1)
    old_probs = (old_weights / totals[..., None]).astype(jnp.bfloat16)
    new_probs = (new_weights / totals[..., None]).astype(jnp.bfloat16)
    attention_mixed_output = jnp.einsum(
        "rgqsl,rlgd->rsgqd", old_probs, stored_entries[:, :, 1], preferred_element_type=jnp.float32
    )
    attention_mixed_output = attention_mixed_output + jnp.einsum(
        "rgqst,rtgd->rsgqd", new_probs, fresh_key_value[1], preferred_element_type=jnp.float32
    )
    return attention_mixed_output.astype(jnp.bfloat16).reshape(
        requests * STEP_COUNT, heads_kv * query_group_count * HEAD_WIDTH
    )


def on_device(
    queries,
    incoming_key_value,
    key_value_pages,
    page_request_home,
    lengths,
    request_adapter_index,
    adapter_storage_slot,
    adapter_down_factor,
    adapter_up_factor,
    output_projection_weight,
):
    req_count = lax.axis_size("req")
    tp_count = lax.axis_size("tp")
    my_req = lax.axis_index("req")
    my_lane = lax.axis_index("tp")
    cache_pages = relocate(key_value_pages, page_request_home, my_req, req_count)
    attention_mixed_output = attend(queries, incoming_key_value, cache_pages, lengths)
    own_tokens = attention_mixed_output.shape[0]
    everyone, adapters = (
        lax.all_gather(attention_mixed_output, "req", axis=0, tiled=True),
        lax.all_gather(request_adapter_index, "req", axis=0, tiled=True),
    )
    slot_count = adapter_storage_slot.shape[0]
    match_table = adapters[:, None] == jnp.arange(slot_count, dtype=jnp.int32)[None, :]
    req_slot = jnp.sum(jnp.where(match_table, adapter_storage_slot[None, :], 0), axis=1)
    token_slot = jnp.repeat(req_slot, STEP_COUNT)
    block_rows = everyone.shape[0] // tp_count
    plain_output_rows = lax.psum_scatter(
        jnp.dot(everyone, output_projection_weight, preferred_element_type=jnp.float32),
        "tp",
        scatter_dimension=0,
        tiled=True,
    )
    gathered_down_factors = lax.all_gather(adapter_down_factor, "req", axis=0, tiled=True)
    local_reduced_rows = jnp.einsum(
        "td,adr->tar",
        attention_mixed_output,
        gathered_down_factors,
        preferred_element_type=jnp.float32,
    )
    own_slot = lax.dynamic_slice_in_dim(token_slot, my_req * own_tokens, own_tokens)
    selected_pages = own_slot[:, None] == jnp.arange(slot_count, dtype=jnp.int32)[None, :]
    adapter_partial = jnp.sum(
        jnp.where(selected_pages[:, :, None], local_reduced_rows, 0.0), axis=1
    )
    distributed_terms = lax.all_gather(adapter_partial, "req", axis=0, tiled=True)
    low_rows = lax.psum_scatter(distributed_terms, "tp", scatter_dimension=0, tiled=True)
    up_factor_columns = lax.all_to_all(
        adapter_up_factor, "req", split_axis=2, concat_axis=0, tiled=True
    )
    low_bf = low_rows.astype(jnp.bfloat16)
    block_slot = lax.dynamic_slice_in_dim(token_slot, my_lane * block_rows, block_rows)
    selector = (block_slot[:, None] == jnp.arange(slot_count, dtype=jnp.int32)[None, :]).astype(
        jnp.bfloat16
    )
    expanded = (selector[:, :, None] * low_bf[:, None, :]).reshape(
        block_rows, slot_count * up_factor_columns.shape[1]
    )
    adapter_output_rows = jnp.dot(
        expanded,
        up_factor_columns.reshape(
            slot_count * up_factor_columns.shape[1], up_factor_columns.shape[2]
        ),
        preferred_element_type=jnp.float32,
    )
    return (plain_output_rows + adapter_output_rows).astype(jnp.bfloat16)


def solution(mesh):
    return jax.shard_map(
        on_device,
        mesh=mesh,
        in_specs=(
            P("req", "tp"),
            P(None, "req", "tp"),
            P("req", None, None, "tp"),
            P("req"),
            P("req"),
            P("req"),
            P(),
            P("req", "tp", None),
            P("req", None, None),
            P("tp", "req"),
        ),
        out_specs=P("tp", "req"),
        check_vma=False,
    )
```

profile of v0, /device:TPU:1, one launch (start us, length us, event | category | flops | bytes accessed | tf_op | source)
XLA Modules:
  0.0 376.8 jit_solution(3903700811539374699)
XLA Ops:
  6.5 0.7 all-gather.6.cloned.1.call-update
  7.3 0.7 subtract_select_fusion
  8.0 1.2 reduce-window.6
  9.1 0.2 slice_reduce_fusion
  9.4 0.1 fusion.20
  9.5 0.1 fusion.17
  9.6 0.8 select_reduce_fusion.4
  10.5 0.7 select_n.130
  11.2 8.6 %all-to-all-start = ((s32[32,2,1]{1,2,0:T(1,128)}), s32[32,2,1]{1,2,0:T(1,128)S(1)}, u32[]{:S(2)}, u32[]{:S(2)}) async-start(s32[32,2,1]{1,2,0:T(1,128)} %bitcast.3), calls=%async_computation | async-start | bytes 32768 | tf_op jit(solution)/shard_map/all_to_all | solution.py:36
  19.8 1.0 copy.36
  20.8 6.0 %gather_fusion = bf16[64,32,2,128]{3,2,1,0:T(2,128)(2,1)S(1)} fusion(bf16[512,32,2,128]{3,2,1,0:T(2,128)(2,1)} %param.12, s32[1024]{0:T(1024)S(1)} %pad_clamp_fusion.1), kind=kCustom, calls=%fused_computation | custom fusion | bytes 2097408 | tf_op jit(solution)/shard_map/jit(_take)/gather | solution.py:31
  26.9 1.4 dynamic-slice
  28.9 0.9 dynamic-update-slice
  29.8 13.7 %all-reduce = s32[1024]{0:T(1024)S(1)} all-reduce(s32[1024]{0:T(1024)S(1)} %dynamic-update-slice), channel_id=1, replica_groups=mesh['req'=32,'tp'=8] {'req'}, use_global_device_ids=true, to_apply=%add | all-reduce | flops 1024 | bytes 8192
  43.5 0.8 select_reduce_fusion.2
  44.3 0.7 iota_compare_fusion.4
  45.0 0.8 fusion.31
  45.8 1.3 fusion.32
  47.1 2.4 broadcast_select_fusion.2
  49.5 0.2 broadcast_in_dim.188
  49.7 0.3 reshape.294
  50.0 0.1 dynamic_slice.7
  50.0 7.1 %all-to-all-start.1 = ((bf16[64,32,2,128]{3,2,1,0:T(2,128)(2,1)}), bf16[64,32,2,128]{3,2,1,0:T(2,128)(2,1)S(1)}, u32[]{:S(2)}, u32[]{:S(2)}) async-start(bf16[64,32,2,128]{3,2,1,0:T(2,128)(2,1)} %broadcast_select_fusion.2), calls=%async_computation.1 | async-start | bytes 2097152 | tf_op jit(solution)/shard_map/all_to_all | solution.py:35
  57.2 0.0 all-gather.8.cloned.1.call-start
  57.2 0.1 fusion.24
  57.3 0.1 select_n.132
  57.4 0.2 select_reduce_fusion.1
  57.6 0.1 reduce_sum.81
  57.7 0.1 broadcast_in_dim.173
  57.9 0.2 broadcast_in_dim.174
  58.0 24.3 %all-to-all-done.1 = bf16[64,32,2,128]{3,2,1,0:T(2,128)(2,1)S(1)} async-done(((bf16[64,32,2,128]{3,2,1,0:T(2,128)(2,1)}), bf16[64,32,2,128]{3,2,1,0:T(2,128)(2,1)S(1)}, u32[]{:S(2)}, u32[]{:S(2)}) %all-to-all-start.1) | async-done | bytes 1048608 | tf_op jit(solution)/shard_map/all_to_all | solution.py:35
  82.3 25.9 %pad_maximum_fusion = bf16[576,32,2,128]{3,2,1,0:T(2,128)(2,1)} fusion(bf16[64,32,2,128]{3,2,1,0:T(2,128)(2,1)S(1)} %all-to-all-done.1, bf16[512,32,2,128]{3,2,1,0:T(2,128)(2,1)} %param.12), kind=kLoop, calls=%fused_computation.2 | loop fusion | flops 4718592 | bytes 18874368 | tf_op jit(solution)/shard_map/concatenate | solution.py:41
  108.2 30.0 %gather_fusion.1 = bf16[512,32,2,128]{3,2,1,0:T(2,128)(2,1)} fusion(bf16[576,32,2,128]{3,2,1,0:T(2,128)(2,1)} %pad_maximum_fusion, s32[1024]{0:T(1024)S(1)} %pad_clamp_fusion), kind=kCustom, calls=%fused_computation.1 | custom fusion | bytes 16779264 | tf_op jit(solution)/shard_map/jit(_take)/gather | solution.py:45
  138.2 7.9 %copy.25 = bf16[512,32,2,128]{3,1,0,2:T(8,128)(2,1)} copy(bf16[512,32,2,128]{3,2,1,0:T(2,128)(2,1)} %gather_fusion.1) | data formatting | bytes 16777216 | tf_op jit(solution)/shard_map/jit(_take)/gather | solution.py:45
  146.1 5.3 %broadcast_select_fusion = bf16[32,512,2,1,128]{4,1,0,3,2:T(8,128)(2,1)S(1)} fusion(bf16[32,512,2,1,128]{4,1,0,3,2:T(8,128)(2,1)} %bitcast.129, pred[32,512]{1,0:T(8,128)(4,1)S(1)} %broadcast_in_dim.174), kind=kLoop, calls=%fused_computation.3 | loop fusion | flops 4194304 | bytes 16793600 | tf_op jit(solution)/shard_map/jit(_take)/select_n | solution.py:45
  151.5 1.6 bitcast_reduce_fusion
  153.1 0.3 fusion.14
  153.3 0.9 fusion.3
  154.2 1.1 fusion.1
  155.4 0.4 fusion.6
  155.7 0.0 all-gather.6.cloned.1.call-done
  155.8 5.8 %fusion.30 = f32[128,4096]{0,1:S(1)} fusion(bf16[1024,4096]{0,1:T(8,128)(2,1)} %bitcast.132, bf16[16,8,8,128]{3,2,1,0:T(8,128)(2,1)S(1)} %bitcast.137), kind=kOutput, calls=%fused_computation.85 | convolution fusion | flops 1073741824 | bytes 10747904
  161.6 0.9 select_reduce_fusion
  162.4 0.0 all-gather.8.cloned.1.call-update
  162.5 0.0 all-gather.4.cloned.1.call-start
  162.5 0.8 copy.41
  163.3 0.0 reduce-scatter.5.cloned.1.call-start
  163.3 45.8 %all-gather.8.cloned.1.call-done = f32[4096,64]{0,1:T(8,128)} async-done(((f32[128,64]{0,1:T(8,128)}), f32[4096,64]{0,1:T(8,128)}) %all-gather.8.cloned.1.call-update) | async-done | bytes 1048592 | tf_op jit(solution)/shard_map/all_gather | solution.py:142
  209.2 0.3 reduce-scatter.3.cloned.1.call-start
  209.5 59.6 %all-gather.4.cloned.1.call-done = bf16[4096,1024]{1,0:T(8,128)(2,1)} async-done(((bf16[128,1024]{1,0:T(8,128)(2,1)}), bf16[4096,1024]{1,0:T(8,128)(2,1)}) %all-gather.4.cloned.1.call-update) | async-done | bytes 8388624 | tf_op jit(solution)/shard_map/all_gather | solution.py:116
  269.0 7.7 %fusion.33 = f32[4096,256]{1,0:T(8,128)} fusion(bf16[4096,1024]{1,0:T(8,128)(2,1)} %all-gather.4.cloned.1.call-done, bf16[1024,256]{1,0:T(8,128)(2,1)S(1)} %copy-done), kind=kOutput, calls=%fused_computation.88 | convolution fusion | flops 2147483648 | bytes 13107200 | tf_op jit(solution)/shard_map/dot_general | solution.py:125
  276.8 1.6 copy-done.1
  278.3 6.9 %copy.26 = bf16[2,64,8192]{1,0,2:T(2,128)(2,1)} copy(bf16[2,64,8192]{2,1,0:T(8,128)(2,1)S(1)} %copy-done.1) | data formatting | bytes 4194304 | tf_op args[8]
  285.2 9.8 %reshape.331 = bf16[32,2,16384]{2,1,0:T(2,128)(2,1)} reshape(bf16[8192,2,64]{2,1,0:T(2,128)(2,1)} %bitcast.131) | data formatting | bytes 4194304
  295.0 5.5 %all-to-all-start.2 = ((bf16[32,2,16384]{2,1,0:T(2,128)(2,1)}), bf16[32,2,16384]{2,1,0:T(2,128)(2,1)S(1)}, u32[]{:S(2)}, u32[]{:S(2)}) async-start(bf16[32,2,16384]{2,1,0:T(2,128)(2,1)} %reshape.331), calls=%async_computation.4 | async-start | bytes 4194304 | tf_op jit(solution)/shard_map/all_to_all | solution.py:144
  300.5 0.1 dynamic_slice.6
  300.6 28.2 %all-to-all-done.2 = bf16[32,2,16384]{2,1,0:T(2,128)(2,1)S(1)} async-done(((bf16[32,2,16384]{2,1,0:T(2,128)(2,1)}), bf16[32,2,16384]{2,1,0:T(2,128)(2,1)S(1)}, u32[]{:S(2)}, u32[]{:S(2)}) %all-to-all-start.2) | async-done | bytes 2097184 | tf_op jit(solution)/shard_map/all_to_all | solution.py:144
  328.9 4.0 %reshape.332 = bf16[8192,2,64]{2,1,0:T(2,128)(2,1)} reshape(bf16[32,2,16384]{2,1,0:T(2,128)(2,1)S(1)} %all-to-all-done.2) | data formatting | bytes 4194304
  332.9 9.3 %copy.34 = bf16[2,64,32,256]{3,1,0,2:T(8,128)(2,1)S(1)} copy(bf16[2,64,32,256]{1,0,3,2:T(2,128)(2,1)} %bitcast.130) | data formatting | bytes 4194304 | tf_op jit(solution)/shard_map/all_to_all | solution.py:144
  342.2 0.0 reduce-scatter.5.cloned.1.call-done
  342.2 0.9 convert_element_type.40
  343.1 2.2 broadcast_multiply_fusion
  345.3 20.7 %reduce-scatter.3.cloned.1.call-done = f32[512,256]{1,0:T(8,128)} async-done(((f32[4096,256]{1,0:T(8,128)}), f32[512,256]{1,0:T(8,128)}) %reduce-scatter.3.cloned.1.call-update) | async-done | bytes 524304 | tf_op jit(solution)/shard_map/reduce_scatter | solution.py:124
  366.0 4.3 %fusion.5 = bf16[512,256]{1,0:T(8,128)(2,1)} fusion(f32[512,256]{1,0:T(8,128)} %reduce-scatter.3.cloned.1.call-done, bf16[512,4096]{0,1:T(8,128)(2,1)} %bitcast.134, bf16[4096,256]{1,0:T(8,128)(2,1)S(1)} %bitcast.135), kind=kOutput, calls=%fused_computation.21 | convolution fusion | flops 1074003968 | bytes 7077888 | tf_op jit(solution)/shard_map/dot_general | solution.py:155
  (26 shorter events, 0.3 us)
Async XLA Ops:
  6.5 262.5 %copy-start = (bf16[1024,256]{1,0:T(8,128)(2,1)S(1)}, bf16[1024,256]{1,0:T(8,128)(2,1)}, u32[]{:S(2)}) copy-start(bf16[1024,256]{1,0:T(8,128)(2,1)} %param.19) | copy-start | bytes 1572868
  6.5 149.2 %all-gather.6.cloned.1.call-start = ((), (), s32[]{:S(2)}) async-start(), calls=%async_computation.7 | async-start | bytes 8650752 | tf_op jit(solution)/shard_map/all_gather | solution.py:130
  11.2 38.8 %all-to-all-start = ((s32[32,2,1]{1,2,0:T(1,128)}), s32[32,2,1]{1,2,0:T(1,128)S(1)}, u32[]{:S(2)}, u32[]{:S(2)}) async-start(s32[32,2,1]{1,2,0:T(1,128)} %bitcast.3), calls=%async_computation | async-start | bytes 32768 | tf_op jit(solution)/shard_map/all_to_all | solution.py:36
  50.0 32.3 %all-to-all-start.1 = ((bf16[64,32,2,128]{3,2,1,0:T(2,128)(2,1)}), bf16[64,32,2,128]{3,2,1,0:T(2,128)(2,1)S(1)}, u32[]{:S(2)}, u32[]{:S(2)}) async-start(bf16[64,32,2,128]{3,2,1,0:T(2,128)(2,1)} %broadcast_select_fusion.2), calls=%async_computation.1 | async-start | bytes 2097152 | tf_op jit(solution)/shard_map/all_to_all | solution.py:35
  57.2 152.0 %all-gather.8.cloned.1.call-start = ((), (), s32[]{:S(2)}) async-start(), calls=%async_computation.8 | async-start | bytes 1081344 | tf_op jit(solution)/shard_map/all_gather | solution.py:142
  162.5 106.6 %all-gather.4.cloned.1.call-start = ((), (), s32[]{:S(2)}) async-start(), calls=%async_computation.5 | async-start | bytes 8650752 | tf_op jit(solution)/shard_map/all_gather | solution.py:116
  163.3 178.9 %reduce-scatter.5.cloned.1.call-start = ((), (), s32[]{:S(2)}) async-start(), calls=%async_computation.9 | async-start | bytes 1179648 | tf_op jit(solution)/shard_map/reduce_scatter | solution.py:143
  209.2 156.8 %reduce-scatter.3.cloned.1.call-start = ((), (), s32[]{:S(2)}) async-start(), calls=%async_computation.6 | async-start | bytes 4718592 | tf_op jit(solution)/shard_map/reduce_scatter | solution.py:124
  276.7 1.6 copy-start.1
  295.0 33.8 %all-to-all-start.2 = ((bf16[32,2,16384]{2,1,0:T(2,128)(2,1)}), bf16[32,2,16384]{2,1,0:T(2,128)(2,1)S(1)}, u32[]{:S(2)}, u32[]{:S(2)}) async-start(bf16[32,2,16384]{2,1,0:T(2,128)(2,1)} %reshape.331), calls=%async_computation.4 | async-start | bytes 4194304 | tf_op jit(solution)/shard_map/all_to_all | solution.py:144
Sparse Core Ops, SparseCore 0:
  9.9 72.5 all-gather.5
  162.6 46.5 all-gather.7
  211.7 57.2 all-gather.3
  271.4 33.2 reduce-scatter.4
  307.1 58.8 reduce-scatter.2
where the time goes:
time: 378 us; the launch traced here: 377 us
  waiting for transfers between devices  179 us (47%)
  local copies, waits for them, and re-layouts  82.3 us (22%)
  other arithmetic  43.6 us (12%)
  matrix products  22.1 us (6%)
  starting transfers between devices  21.6 us (6%)
  between operations  14.1 us (4%)
  blocking collectives  13.7 us (4%)
    all_gather x1, waiting for transfers between devices, on_device(): lax.all_gather(attention_mixed_output, 'req', axis=0, tiled=True)  59.6 us
    all_gather x1, waiting for transfers between devices, on_device(): lax.all_gather(adapter_partial, 'req', axis=0, tiled=True)  45.8 us
    gather x2, local copies, waits for them, and re-layouts, relocate(): return jnp.take(candidates, slot_source, axis=0)  37.9 us
    all_to_all x1, waiting for transfers between devices, on_device(): lax.all_to_all(adapter_up_factor, 'req', split_axis=2, concat_axis=0, til...  28.2 us
    unnamed x12, local copies, waits for them, and re-layouts  26.2 us
    concatenate x1, other arithmetic, relocate(): candidates = jnp.concatenate([key_value_pages, inbox_pages], axis=0)  25.9 us
    all_to_all x1, waiting for transfers between devices, relocate(): lax.all_to_all(outbox, 'req', split_axis=0, concat_axis=0, tiled=True)  24.3 us
    reduce_scatter x1, waiting for transfers between devices, on_device(): lax.psum_scatter(jnp.dot(everyone, output_projection_weight, preferred_el...  20.7 us
  transfers between devices with their start and end apart: 8, of which 5 were waited for; matrix products, arithmetic and copies ran while one was open for 36% of the time, Pallas kernels for 0%

commit v1 on v0

--- a/solution.py
+++ b/solution.py
@@ -139,7 +139,10 @@
     adapter_partial = jnp.sum(
         jnp.where(selected_pages[:, :, None], local_reduced_rows, 0.0), axis=1
     )
-    distributed_terms = lax.all_gather(adapter_partial, "req", axis=0, tiled=True)
+    size = lax.axis_size("req")
+    parts = jnp.stack([adapter_partial for _ in range(size)])
+    parts = lax.all_to_all(parts, "req", split_axis=0, concat_axis=0)
+    distributed_terms = jnp.concatenate(parts, axis=0)
     low_rows = lax.psum_scatter(distributed_terms, "tp", scatter_dimension=0, tiled=True)
     up_factor_columns = lax.all_to_all(
         adapter_up_factor, "req", split_axis=2, concat_axis=0, tiled=True

time: 378 us -> 303 us (0.80)
  waiting for transfers between devices: 179 us -> 85.4 us
  blocking collectives: 13.7 us -> 36 us
    all_gather x1 -> x0, waiting for transfers between devices: 45.8 us -> none  [on_device(): lax.all_gather(adapter_partial, 'req', axis=0, tiled=True)]
    all_gather x1, waiting for transfers between devices: 59.6 us -> 16.5 us  [on_device(): lax.all_gather(attention_mixed_output, 'req', axis=0, tiled=True)]
    all_to_all x0 -> x1, blocking collectives: none -> 24.9 us  [on_device(): parts = lax.all_to_all(parts, 'req', split_axis=0, concat_axis=0)]
    all_to_all x1, waiting for transfers between devices: 24.3 us -> 16 us  [relocate(): lax.all_to_all(outbox, 'req', split_axis=0, concat_axis=0, tiled=True)]
    unnamed x12 -> x20, local copies, waits for them, and re-layouts: 26.2 us -> 24.8 us
  transfers between devices with their start and end apart: 8 -> 7, of which waited for: 5 -> 4; matrix products, arithmetic and copies ran while one was open for 36% -> 46% of each run, Pallas kernels for 0% -> 0%
where the time goes in v1:
time: 303 us; the launch traced here: 302 us
  waiting for transfers between devices  85.4 us (28%)
  local copies, waits for them, and re-layouts  82.2 us (27%)
  other arithmetic  41.6 us (14%)
  blocking collectives  36 us (12%)
  matrix products  22.4 us (7%)
  starting transfers between devices  20.6 us (7%)
  between operations  14 us (5%)
    gather x2, local copies, waits for them, and re-layouts, relocate(): return jnp.take(candidates, slot_source, axis=0)  37.9 us
    all_to_all x1, waiting for transfers between devices, on_device(): lax.all_to_all(adapter_up_factor, 'req', split_axis=2, concat_axis=0, til...  28.2 us
    concatenate x1, other arithmetic, relocate(): candidates = jnp.concatenate([key_value_pages, inbox_pages], axis=0)  25.9 us
    all_to_all x1, blocking collectives, on_device(): parts = lax.all_to_all(parts, 'req', split_axis=0, concat_axis=0)  24.9 us
    unnamed x20, local copies, waits for them, and re-layouts  24.8 us
    reduce_scatter x1, waiting for transfers between devices, on_device(): lax.psum_scatter(jnp.dot(everyone, output_projection_weight, preferred_el...  23.8 us
    all_gather x1, waiting for transfers between devices, on_device(): lax.all_gather(attention_mixed_output, 'req', axis=0, tiled=True)  16.5 us
    all_to_all x1, waiting for transfers between devices, relocate(): lax.all_to_all(outbox, 'req', split_axis=0, concat_axis=0, tiled=True)  16 us
  transfers between devices with their start and end apart: 7, of which 4 were waited for; matrix products, arithmetic and copies ran while one was open for 46% of the time, Pallas kernels for 0%

profile of v1, /device:TPU:1, one launch (start us, length us, event | category | flops | bytes accessed | tf_op | source)
XLA Modules:
  0.0 302.2 jit_solution(6709512376872074682)
XLA Ops:
  6.5 0.7 all-gather.5.cloned.1.call-update
  7.3 0.7 subtract_select_fusion
  8.0 1.2 reduce-window.6
  9.1 0.2 slice_reduce_fusion
  9.4 0.1 fusion.20
  9.5 0.1 fusion.17
  9.6 0.8 select_reduce_fusion.4
  10.5 0.7 select_n.130
  11.2 8.6 %all-to-all-start = ((s32[32,2,1]{1,2,0:T(1,128)}), s32[32,2,1]{1,2,0:T(1,128)S(1)}, u32[]{:S(2)}, u32[]{:S(2)}) async-start(s32[32,2,1]{1,2,0:T(1,128)} %bitcast.3), calls=%async_computation | async-start | bytes 32768 | tf_op jit(solution)/shard_map/all_to_all | solution.py:36
  19.8 1.0 copy.45
  20.8 6.0 %gather_fusion = bf16[64,32,2,128]{3,2,1,0:T(2,128)(2,1)S(1)} fusion(bf16[512,32,2,128]{3,2,1,0:T(2,128)(2,1)} %param.12, s32[1024]{0:T(1024)S(1)} %pad_clamp_fusion.1), kind=kCustom, calls=%fused_computation | custom fusion | bytes 2097408 | tf_op jit(solution)/shard_map/jit(_take)/gather | solution.py:31
  26.9 0.8 fusion.31
  27.7 2.4 broadcast_select_fusion.2
  30.1 1.3 fusion.32
  31.3 7.4 %all-to-all-start.1 = ((bf16[64,32,2,128]{3,2,1,0:T(2,128)(2,1)}), bf16[64,32,2,128]{3,2,1,0:T(2,128)(2,1)S(1)}, u32[]{:S(2)}, u32[]{:S(2)}) async-start(bf16[64,32,2,128]{3,2,1,0:T(2,128)(2,1)} %broadcast_select_fusion.2), calls=%async_computation.1 | async-start | bytes 2097152 | tf_op jit(solution)/shard_map/all_to_all | solution.py:35
  38.7 0.2 all-gather.3.cloned.1.call-start
  39.0 0.1 iota_compare_fusion.4
  39.1 0.1 fusion.24
  39.1 0.1 select_n.132
  39.3 0.2 select_reduce_fusion.1
  39.5 0.1 reduce_sum.81
  39.6 0.1 broadcast_in_dim.173
  39.7 0.2 broadcast_in_dim.174
  39.9 16.0 %all-to-all-done.1 = bf16[64,32,2,128]{3,2,1,0:T(2,128)(2,1)S(1)} async-done(((bf16[64,32,2,128]{3,2,1,0:T(2,128)(2,1)}), bf16[64,32,2,128]{3,2,1,0:T(2,128)(2,1)S(1)}, u32[]{:S(2)}, u32[]{:S(2)}) %all-to-all-start.1) | async-done | bytes 1048608 | tf_op jit(solution)/shard_map/all_to_all | solution.py:35
  55.9 25.9 %pad_maximum_fusion = bf16[576,32,2,128]{3,2,1,0:T(2,128)(2,1)} fusion(bf16[64,32,2,128]{3,2,1,0:T(2,128)(2,1)S(1)} %all-to-all-done.1, bf16[512,32,2,128]{3,2,1,0:T(2,128)(2,1)} %param.12), kind=kLoop, calls=%fused_computation.2 | loop fusion | flops 4718592 | bytes 18874368 | tf_op jit(solution)/shard_map/concatenate | solution.py:41
  81.7 30.0 %gather_fusion.1 = bf16[512,32,2,128]{3,2,1,0:T(2,128)(2,1)} fusion(bf16[576,32,2,128]{3,2,1,0:T(2,128)(2,1)} %pad_maximum_fusion, s32[1024]{0:T(1024)S(1)} %pad_clamp_fusion), kind=kCustom, calls=%fused_computation.1 | custom fusion | bytes 16779264 | tf_op jit(solution)/shard_map/jit(_take)/gather | solution.py:45
  111.8 7.9 %copy.32 = bf16[512,32,2,128]{3,1,0,2:T(8,128)(2,1)} copy(bf16[512,32,2,128]{3,2,1,0:T(2,128)(2,1)} %gather_fusion.1) | data formatting | bytes 16777216 | tf_op jit(solution)/shard_map/jit(_take)/gather | solution.py:45
  119.7 5.3 %broadcast_select_fusion = bf16[32,512,2,1,128]{4,1,0,3,2:T(8,128)(2,1)S(1)} fusion(bf16[32,512,2,1,128]{4,1,0,3,2:T(8,128)(2,1)} %bitcast.134, pred[32,512]{1,0:T(8,128)(4,1)S(1)} %broadcast_in_dim.174), kind=kLoop, calls=%fused_computation.3 | loop fusion | flops 4194304 | bytes 16793600 | tf_op jit(solution)/shard_map/jit(_take)/select_n | solution.py:45
  125.0 1.6 bitcast_reduce_fusion
  126.6 0.3 fusion.14
  126.9 0.9 fusion.3
  127.8 1.1 fusion.1
  128.9 0.4 fusion.6
  129.3 0.8 copy.51
  130.1 0.0 reduce-scatter.5.cloned.1.call-start
  130.1 0.6 dynamic-slice
  131.3 0.2 dynamic-update-slice
  131.5 11.0 %all-reduce = s32[1024]{0:T(1024)S(1)} all-reduce(s32[1024]{0:T(1024)S(1)} %dynamic-update-slice), channel_id=1, replica_groups=mesh['req'=32,'tp'=8] {'req'}, use_global_device_ids=true, to_apply=%add | all-reduce | flops 1024 | bytes 8192
  142.6 0.1 select_reduce_fusion.2
  142.7 0.2 broadcast_in_dim.188
  142.9 0.3 reshape.299
  143.1 0.1 dynamic_slice.7
  143.2 0.0 all-gather.5.cloned.1.call-done
  143.3 6.1 %fusion.30 = f32[128,4096]{0,1:S(1)} fusion(bf16[1024,4096]{0,1:T(8,128)(2,1)} %bitcast.137, bf16[16,8,8,128]{3,2,1,0:T(8,128)(2,1)S(1)} %bitcast.143), kind=kOutput, calls=%fused_computation.86 | convolution fusion | flops 1073741824 | bytes 10747904
  149.3 0.3 select_reduce_fusion
  149.6 0.1 stack.2
  149.7 24.9 %all_to_all.31 = f32[32,128,64]{1,2,0:T(8,128)S(1)} all-to-all(f32[32,128,64]{1,2,0:T(8,128)S(1)} %stack.2), channel_id=1, replica_groups=mesh['req'=32,'tp'=8] {'req'}, dimensions={0} | all-to-all | bytes 2097152 | tf_op jit(solution)/shard_map/all_to_all | solution.py:144
  174.7 1.1 copy_bitcast_fusion
  175.8 0.0 reduce-scatter.3.cloned.1.call-start
  175.9 16.5 %all-gather.3.cloned.1.call-done = bf16[4096,1024]{1,0:T(8,128)(2,1)} async-done(((bf16[128,1024]{1,0:T(8,128)(2,1)}), bf16[4096,1024]{1,0:T(8,128)(2,1)}) %all-gather.3.cloned.1.call-update) | async-done | bytes 8388624 | tf_op jit(solution)/shard_map/all_gather | solution.py:116
  192.4 7.7 %fusion.33 = f32[4096,256]{1,0:T(8,128)} fusion(bf16[4096,1024]{1,0:T(8,128)(2,1)} %all-gather.3.cloned.1.call-done, bf16[1024,256]{1,0:T(8,128)(2,1)S(1)} %copy-done), kind=kOutput, calls=%fused_computation.89 | convolution fusion | flops 2147483648 | bytes 13107200 | tf_op jit(solution)/shard_map/dot_general | solution.py:125
  200.1 1.6 copy-done.1
  201.7 6.9 %copy.34 = bf16[2,64,8192]{1,0,2:T(2,128)(2,1)} copy(bf16[2,64,8192]{2,1,0:T(8,128)(2,1)S(1)} %copy-done.1) | data formatting | bytes 4194304 | tf_op args[8]
  208.6 9.8 %reshape.337 = bf16[32,2,16384]{2,1,0:T(2,128)(2,1)} reshape(bf16[8192,2,64]{2,1,0:T(2,128)(2,1)} %bitcast.136) | data formatting | bytes 4194304
  218.4 4.3 %all-to-all-start.3 = ((bf16[32,2,16384]{2,1,0:T(2,128)(2,1)}), bf16[32,2,16384]{2,1,0:T(2,128)(2,1)S(1)}, u32[]{:S(2)}, u32[]{:S(2)}) async-start(bf16[32,2,16384]{2,1,0:T(2,128)(2,1)} %reshape.337), calls=%async_computation.5 | async-start | bytes 4194304 | tf_op jit(solution)/shard_map/all_to_all | solution.py:147
  222.7 0.1 dynamic_slice.6
  222.8 28.2 %all-to-all-done.3 = bf16[32,2,16384]{2,1,0:T(2,128)(2,1)S(1)} async-done(((bf16[32,2,16384]{2,1,0:T(2,128)(2,1)}), bf16[32,2,16384]{2,1,0:T(2,128)(2,1)S(1)}, u32[]{:S(2)}, u32[]{:S(2)}) %all-to-all-start.3) | async-done | bytes 2097184 | tf_op jit(solution)/shard_map/all_to_all | solution.py:147
  251.0 4.0 %reshape.338 = bf16[8192,2,64]{2,1,0:T(2,128)(2,1)} reshape(bf16[32,2,16384]{2,1,0:T(2,128)(2,1)S(1)} %all-to-all-done.3) | data formatting | bytes 4194304
  255.0 9.3 %copy.42 = bf16[2,64,32,256]{3,1,0,2:T(8,128)(2,1)S(1)} copy(bf16[2,64,32,256]{1,0,3,2:T(2,128)(2,1)} %bitcast.135) | data formatting | bytes 4194304 | tf_op jit(solution)/shard_map/all_to_all | solution.py:147
  264.3 0.0 reduce-scatter.5.cloned.1.call-done
  264.4 0.9 convert_element_type.40
  265.3 2.2 broadcast_multiply_fusion
  267.5 23.8 %reduce-scatter.3.cloned.1.call-done = f32[512,256]{1,0:T(8,128)} async-done(((f32[4096,256]{1,0:T(8,128)}), f32[512,256]{1,0:T(8,128)}) %reduce-scatter.3.cloned.1.call-update) | async-done | bytes 524304 | tf_op jit(solution)/shard_map/reduce_scatter | solution.py:124
  291.3 4.3 %fusion.5 = bf16[512,256]{1,0:T(8,128)(2,1)} fusion(f32[512,256]{1,0:T(8,128)} %reduce-scatter.3.cloned.1.call-done, bf16[512,4096]{0,1:T(8,128)(2,1)} %bitcast.139, bf16[4096,256]{1,0:T(8,128)(2,1)S(1)} %bitcast.140), kind=kOutput, calls=%fused_computation.21 | convolution fusion | flops 1074003968 | bytes 7077888 | tf_op jit(solution)/shard_map/dot_general | solution.py:158
  (34 shorter events, 0.3 us)
Async XLA Ops:
  6.5 185.9 %copy-start = (bf16[1024,256]{1,0:T(8,128)(2,1)S(1)}, bf16[1024,256]{1,0:T(8,128)(2,1)}, u32[]{:S(2)}) copy-start(bf16[1024,256]{1,0:T(8,128)(2,1)} %param.19) | copy-start | bytes 1572868
  6.5 32.4 %copy-start.2 = (s32[32]{0:T(128)S(1)}, s32[32]{0:T(128)}, u32[]{:S(2)}) copy-start(s32[32]{0:T(128)} %param.14) | copy-start | bytes 388
  6.5 136.7 %all-gather.5.cloned.1.call-start = ((), (), s32[]{:S(2)}) async-start(), calls=%async_computation.8 | async-start | bytes 8650752 | tf_op jit(solution)/shard_map/all_gather | solution.py:130
  11.2 20.1 %all-to-all-start = ((s32[32,2,1]{1,2,0:T(1,128)}), s32[32,2,1]{1,2,0:T(1,128)S(1)}, u32[]{:S(2)}, u32[]{:S(2)}) async-start(s32[32,2,1]{1,2,0:T(1,128)} %bitcast.3), calls=%async_computation | async-start | bytes 32768 | tf_op jit(solution)/shard_map/all_to_all | solution.py:36
  31.3 24.5 %all-to-all-start.1 = ((bf16[64,32,2,128]{3,2,1,0:T(2,128)(2,1)}), bf16[64,32,2,128]{3,2,1,0:T(2,128)(2,1)S(1)}, u32[]{:S(2)}, u32[]{:S(2)}) async-start(bf16[64,32,2,128]{3,2,1,0:T(2,128)(2,1)} %broadcast_select_fusion.2), calls=%async_computation.1 | async-start | bytes 2097152 | tf_op jit(solution)/shard_map/all_to_all | solution.py:35
  38.7 153.7 %all-gather.3.cloned.1.call-start = ((), (), s32[]{:S(2)}) async-start(), calls=%async_computation.6 | async-start | bytes 8650752 | tf_op jit(solution)/shard_map/all_gather | solution.py:116
  127.8 2.4 copy-start.5
  127.8 3.5 %copy-start.4 = (s32[32]{0:T(128)S(1)}, s32[32]{0:T(128)}, u32[]{:S(2)}) copy-start(s32[32]{0:T(128)} %param.15) | copy-start | bytes 388
  127.8 14.8 %copy-start.3 = (s32[64]{0:T(128)S(1)}, s32[64]{0:T(128)}, u32[]{:S(2)}) copy-start(s32[64]{0:T(128)} %param.16) | copy-start | bytes 772
  130.1 134.3 %reduce-scatter.5.cloned.1.call-start = ((), (), s32[]{:S(2)}) async-start(), calls=%async_computation.9 | async-start | bytes 1179648 | tf_op jit(solution)/shard_map/reduce_scatter | solution.py:146
  175.8 115.5 %reduce-scatter.3.cloned.1.call-start = ((), (), s32[]{:S(2)}) async-start(), calls=%async_computation.7 | async-start | bytes 4718592 | tf_op jit(solution)/shard_map/reduce_scatter | solution.py:124
  200.1 1.6 copy-start.1
  218.4 32.6 %all-to-all-start.3 = ((bf16[32,2,16384]{2,1,0:T(2,128)(2,1)}), bf16[32,2,16384]{2,1,0:T(2,128)(2,1)S(1)}, u32[]{:S(2)}, u32[]{:S(2)}) async-start(bf16[32,2,16384]{2,1,0:T(2,128)(2,1)} %reshape.337), calls=%async_computation.5 | async-start | bytes 4194304 | tf_op jit(solution)/shard_map/all_to_all | solution.py:147
Sparse Core Ops, SparseCore 0:
  9.9 63.9 all-gather.4
  130.2 62.1 all-gather.2
  194.9 35.2 reduce-scatter.4
  232.7 58.6 reduce-scatter.2
